TPU v7x, 32 devices: a whole 2x2x4 slice. The times are simulated.
32 devices in a mesh: dp: 2 (over x), row: 4 (over z), col: 4 (over y, core).
Axes of the slice: x: 2, y: 2, z: 4, core: 2. Of those that a mesh axis runs over, the one named last changes fastest.
Arguments:
- tokens: bfloat16 [2, 768, 4096], P(None, 'row', ('dp', 'col')), may hold values from -6 to 6
- w_query: bfloat16 [768, 768], P(('row', 'dp'), 'col'), may hold values from -0.21875 to 0.21875
- w_key: bfloat16 [768, 768], P(('row', 'dp'), 'col'), may hold values from -0.21875 to 0.21875
- w_value: bfloat16 [768, 768], P(('row', 'dp'), 'col'), may hold values from -0.21875 to 0.21875
- w_output: bfloat16 [768, 768], P(('col', 'dp'), 'row'), may hold values from -6 to 6
- w_inner: bfloat16 [768, 3072], P(('row', 'dp'), 'col'), may hold values from -0.21875 to 0.21875
- w_outer: bfloat16 [3072, 768], P(('col', 'dp'), 'row'), may hold values from -0.109375 to 0.109375
- first_gain: float32 [768], P('row'), may hold values from 0.1 to 1.9
- first_shift: float32 [768], P('row'), may hold values from -3 to 3
- second_gain: float32 [768], P('row'), may hold values from 0.1 to 1.9
- second_shift: float32 [768], P('row'), may hold values from -3 to 3
- seq_lengths: int32 [2, 2], replicated, may hold values from 512 to 2048, as said below
- out_grad: bfloat16 [2, 768, 4096], P(None, 'row', ('dp', 'col')), may hold values from -6 to 6
Outputs:
- mixed: bfloat16 [2, 768, 4096], P(None, 'row', ('dp', 'col'))
- d_input: float32 [2, 768, 4096], P(None, 'row', ('dp', 'col'))
- grad_w_query: float32 [768, 768], P(('row', 'dp'), 'col')
- grad_w_key: float32 [768, 768], P(('row', 'dp'), 'col')
- grad_w_value: float32 [768, 768], P(('row', 'dp'), 'col')
- grad_w_output: float32 [768, 768], P(('col', 'dp'), 'row')
- grad_w_inner: float32 [768, 3072], P(('row', 'dp'), 'col')
- grad_w_outer: float32 [3072, 768], P(('col', 'dp'), 'row')
- grad_first_gain: float32 [768], P('row')
- grad_first_shift: float32 [768], P('row')
- grad_second_gain: float32 [768], P('row')
- grad_second_shift: float32 [768], P('row')
Inputs may be any that keep to these rules, and one draw needn't show every extreme that they name: micro-batch m's sequence in data group g fills the first seq_lengths[m, g] positions of the group's slot of 2048 token slots; in every draw some sequence has exactly 2048 tokens and some exactly 512.
All inputs are finite; a program needn't handle non-finite values.
Results may differ from a plain program's by a relative error of at most 0.02.
Values may be sent and summed in bfloat16 or wider, within the bound.
No kernel may reach another device: no remote copies, remote signals or barrier semaphores. Data moves between devices by JAX's collectives and lax.ppermute only.
A program may use at most 128 MiB of HBM per device.

v0:
```python
import jax
import jax.numpy as jnp
from jax import lax
from jax.sharding import PartitionSpec as P

HD = 64
norm_eps = 1e-05
masked_score = -1e30


def rotate_pairs(values, positions, head_size, direction):
    row_count = values.shape[0]
    row_width = values.shape[1]
    half_size = head_size // 2
    frequency = 10000.0 ** (-2.0 * jnp.arange(half_size, dtype=jnp.float32) / head_size)
    angles = positions.astype(jnp.float32)[:, None] * frequency[None, :]
    cosine = jnp.cos(angles)[:, None, :]
    sine_part = direction * jnp.sin(angles)[:, None, :]
    paired = values.reshape(row_count, row_width // head_size, half_size, 2)
    even_part = paired[..., 0]
    odd_part = paired[..., 1]
    turned = jnp.stack(
        [even_part * cosine - odd_part * sine_part, even_part * sine_part + odd_part * cosine],
        axis=-1,
    )
    return turned.reshape(row_count, row_width)


def fetch_blocks(w_query, w_key, w_value, w_output, w_inner, w_outer):
    return (
        lax.all_gather(w_query, "dp", axis=0, tiled=True),
        lax.all_gather(w_key, "dp", axis=0, tiled=True),
        lax.all_gather(w_value, "dp", axis=0, tiled=True),
        lax.all_gather(w_output, "dp", axis=0, tiled=True),
        lax.all_gather(w_inner, "dp", axis=0, tiled=True),
        lax.all_gather(w_outer, "dp", axis=0, tiled=True),
    )


def along_col(values):
    return lax.all_gather(values, "col", axis=0, tiled=True)


def along_row(values):
    return lax.all_gather(values, "row", axis=0, tiled=True)


def reduce_rows(values):
    return lax.psum_scatter(values, "row", scatter_dimension=0, tiled=True)


def reduce_cols(values):
    return lax.psum_scatter(
        values.astype(jnp.bfloat16), "col", scatter_dimension=0, tiled=True
    ).astype(jnp.float32)


def feature_totals(first_sum, second_sum):
    return lax.psum((first_sum, second_sum), "row")


def contract_rows(left, right):
    return lax.dot_general(
        left, right, (((0,), (0,)), ((), ())), preferred_element_type=jnp.float32
    )


def times_transpose(left, right):
    return lax.dot_general(
        left, right, (((1,), (1,)), ((), ())), preferred_element_type=jnp.float32
    )


def layer_norm(summed, gain_vec, shift_vec, full_width):
    first_sum, second_sum = feature_totals(
        jnp.sum(summed, axis=1), jnp.sum(summed * summed, axis=1)
    )
    row_mean = first_sum / full_width
    row_var = second_sum / full_width - row_mean * row_mean
    inv_scale = lax.rsqrt(row_var + norm_eps)
    centered = (summed - row_mean[:, None]) * inv_scale[:, None]
    return (centered * gain_vec + shift_vec, centered, inv_scale)


def layer_norm_back(grad_out, centered, inv_scale, gain_vec, full_width):
    grad_cent = grad_out * gain_vec
    first_sum, second_sum = feature_totals(
        jnp.sum(grad_cent, axis=1), jnp.sum(grad_cent * centered, axis=1)
    )
    return inv_scale[:, None] * (
        grad_cent - first_sum[:, None] / full_width - centered * (second_sum / full_width)[:, None]
    )


def split_heads(values, head_size):
    row_count = values.shape[0]
    return values.reshape(row_count, values.shape[1] // head_size, head_size).transpose(1, 0, 2)


def merge_heads(values):
    return values.transpose(1, 0, 2).reshape(values.shape[1], values.shape[0] * values.shape[2])


def attend_forward(query_heads, key_heads, value_heads, key_valid, score_scale):

    def one_head(head_items):
        query_rows, key_rows, value_rows = head_items
        scores = times_transpose(query_rows, key_rows) * score_scale
        scores = jnp.where(key_valid[None, :], scores, masked_score)
        row_top = jnp.max(scores, axis=1, keepdims=True)
        row_total = jnp.sum(jnp.exp(scores - row_top), axis=1, keepdims=True)
        log_total = row_top + jnp.log(row_total)
        probs_low = jnp.exp(scores - log_total).astype(jnp.bfloat16)
        head_out = jnp.dot(probs_low, value_rows, preferred_element_type=jnp.float32)
        return (head_out, log_total[:, 0])

    return lax.map(one_head, (query_heads, key_heads, value_heads))


def attend_backward(
    query_heads, key_heads, value_heads, log_totals, grad_heads, key_valid, score_scale
):

    def one_head(head_items):
        query_rows, key_rows, value_rows, log_total, grad_rows = head_items
        scores = times_transpose(query_rows, key_rows) * score_scale
        scores = jnp.where(key_valid[None, :], scores, masked_score)
        probs_full = jnp.exp(scores - log_total[:, None])
        grad_probs = times_transpose(grad_rows, value_rows)
        row_delta = jnp.sum(probs_full * grad_probs, axis=1, keepdims=True)
        grad_scores = (probs_full * (grad_probs - row_delta)).astype(jnp.bfloat16)
        grad_query = (
            jnp.dot(grad_scores, key_rows, preferred_element_type=jnp.float32) * score_scale
        )
        grad_key = contract_rows(grad_scores, query_rows) * score_scale
        grad_value = contract_rows(probs_full.astype(jnp.bfloat16), grad_rows)
        return (grad_query, grad_key, grad_value)

    return lax.map(one_head, (query_heads, key_heads, value_heads, log_totals, grad_heads))


def gelu_exact(values):
    return jax.nn.gelu(values, approximate=False)


def local(
    tokens,
    w_query,
    w_key,
    w_value,
    w_output,
    w_inner,
    w_outer,
    first_gain,
    first_shift,
    second_gain,
    second_shift,
    seq_lengths,
    out_grad,
):
    micro_count = tokens.shape[0]
    feat_a = tokens.shape[1]
    rows_a = tokens.shape[2]
    count_col = lax.axis_size("col")
    count_row = lax.axis_size("row")
    seq_total = rows_a * count_col
    rows_b = seq_total // count_row
    full_width = feat_a * count_row
    head_size = HD
    score_scale = head_size ** (-0.5)
    width_b = w_query.shape[1]
    inner_width = w_inner.shape[1]
    group_index = lax.axis_index("dp")
    pos_a = lax.axis_index("col") * rows_a + jnp.arange(rows_a, dtype=jnp.int32)
    pos_b = lax.axis_index("row") * rows_b + jnp.arange(rows_b, dtype=jnp.int32)
    pos_all = jnp.arange(seq_total, dtype=jnp.int32)
    acc_qkv = jnp.zeros((feat_a, 3 * width_b), jnp.float32)
    acc_output = jnp.zeros((width_b, feat_a), jnp.float32)
    acc_inner = jnp.zeros((feat_a, inner_width), jnp.float32)
    acc_outer = jnp.zeros((inner_width, feat_a), jnp.float32)
    acc_gain_one = jnp.zeros((feat_a,), jnp.float32)
    acc_shift_one = jnp.zeros((feat_a,), jnp.float32)
    acc_gain_two = jnp.zeros((feat_a,), jnp.float32)
    acc_shift_two = jnp.zeros((feat_a,), jnp.float32)
    outputs = []
    input_grads = []
    for micro_step in range(micro_count):
        forward_blocks = fetch_blocks(w_query, w_key, w_value, w_output, w_inner, w_outer)
        query_block, key_block, value_block, output_block, inner_block, outer_block = forward_blocks
        length_now = lax.dynamic_index_in_dim(seq_lengths[micro_step], group_index, keepdims=False)
        valid_a = pos_a < length_now
        key_valid = pos_all < length_now
        tokens_now = tokens[micro_step].T
        tokens_all = along_col(tokens_now)
        qkv_block = jnp.concatenate([query_block, key_block, value_block], axis=1)
        projected = reduce_rows(jnp.dot(tokens_all, qkv_block, preferred_element_type=jnp.float32))
        query_rot = rotate_pairs(projected[:, :width_b], pos_b, head_size, 1.0).astype(jnp.bfloat16)
        key_rot = rotate_pairs(projected[:, width_b : 2 * width_b], pos_b, head_size, 1.0).astype(
            jnp.bfloat16
        )
        value_low = projected[:, 2 * width_b :].astype(jnp.bfloat16)
        key_all, value_all = (
            lax.all_gather(key_rot, "row", axis=0, tiled=True),
            lax.all_gather(value_low, "row", axis=0, tiled=True),
        )
        query_heads = split_heads(query_rot, head_size)
        head_outs, log_totals = attend_forward(
            query_heads,
            split_heads(key_all, head_size),
            split_heads(value_all, head_size),
            key_valid,
            score_scale,
        )
        attn_low = merge_heads(head_outs).astype(jnp.bfloat16)
        attn_all = along_row(attn_low)
        branch = reduce_cols(jnp.dot(attn_all, output_block, preferred_element_type=jnp.float32))
        hidden, centered_one, inv_one = layer_norm(
            tokens_now.astype(jnp.float32) + branch, first_gain, first_shift, full_width
        )
        hidden_all = along_col(hidden.astype(jnp.bfloat16))
        inner = reduce_rows(jnp.dot(hidden_all, inner_block, preferred_element_type=jnp.float32))
        act_low = gelu_exact(inner).astype(jnp.bfloat16)
        act_all = along_row(act_low)
        outer = reduce_cols(jnp.dot(act_all, outer_block, preferred_element_type=jnp.float32))
        result, centered_two, inv_two = layer_norm(
            hidden + outer, second_gain, second_shift, full_width
        )
        outputs.append(result.astype(jnp.bfloat16).T)
        backward_blocks = fetch_blocks(w_query, w_key, w_value, w_output, w_inner, w_outer)
        query_back, key_block_back, value_back, output_back, inner_back, outer_back = (
            backward_blocks
        )
        qkv_back = jnp.concatenate([query_back, key_block_back, value_back], axis=1)
        cot_now = out_grad[micro_step].T.astype(jnp.float32) * valid_a[:, None].astype(jnp.float32)
        acc_gain_two = acc_gain_two + jnp.sum(cot_now * centered_two, axis=0)
        acc_shift_two = acc_shift_two + jnp.sum(cot_now, axis=0)
        grad_two = layer_norm_back(cot_now, centered_two, inv_two, second_gain, full_width)
        outer_all = along_col(grad_two.astype(jnp.bfloat16))
        grad_act = reduce_rows(times_transpose(outer_all, outer_back))
        acc_outer = acc_outer + contract_rows(act_all, outer_all)
        gelu_pull = jax.vjp(gelu_exact, inner)[1]
        inner_low = gelu_pull(grad_act)[0].astype(jnp.bfloat16)
        inner_all = along_row(inner_low)
        grad_hidden = grad_two + reduce_cols(times_transpose(inner_all, inner_back))
        acc_inner = acc_inner + contract_rows(hidden_all, inner_all)
        acc_gain_one = acc_gain_one + jnp.sum(grad_hidden * centered_one, axis=0)
        acc_shift_one = acc_shift_one + jnp.sum(grad_hidden, axis=0)
        grad_one = layer_norm_back(grad_hidden, centered_one, inv_one, first_gain, full_width)
        branch_all = along_col(grad_one.astype(jnp.bfloat16))
        grad_attn = reduce_rows(times_transpose(branch_all, output_back))
        acc_output = acc_output + contract_rows(attn_all, branch_all)
        key_again, value_again = (
            lax.all_gather(key_rot, "row", axis=0, tiled=True),
            lax.all_gather(value_low, "row", axis=0, tiled=True),
        )
        grad_q_heads, grad_k_heads, grad_v_heads = attend_backward(
            query_heads,
            split_heads(key_again, head_size),
            split_heads(value_again, head_size),
            log_totals,
            split_heads(grad_attn.astype(jnp.bfloat16), head_size),
            key_valid,
            score_scale,
        )
        key_sum, value_sum = (
            lax.psum_scatter(
                merge_heads(grad_k_heads).astype(jnp.bfloat16),
                "row",
                scatter_dimension=0,
                tiled=True,
            ).astype(jnp.float32),
            lax.psum_scatter(
                merge_heads(grad_v_heads).astype(jnp.bfloat16),
                "row",
                scatter_dimension=0,
                tiled=True,
            ).astype(jnp.float32),
        )
        grad_query = rotate_pairs(merge_heads(grad_q_heads), pos_b, head_size, -1.0).astype(
            jnp.bfloat16
        )
        grad_key = rotate_pairs(key_sum, pos_b, head_size, -1.0).astype(jnp.bfloat16)
        grad_value = value_sum.astype(jnp.bfloat16)
        proj_all = along_row(jnp.concatenate([grad_query, grad_key, grad_value], axis=1))
        input_grads.append((grad_one + reduce_cols(times_transpose(proj_all, qkv_back))).T)
        acc_qkv = acc_qkv + contract_rows(tokens_all, proj_all)
    grad_parts = (
        lax.psum_scatter(
            acc_qkv[:, :width_b].astype(jnp.bfloat16), "dp", scatter_dimension=0, tiled=True
        ).astype(jnp.float32),
        lax.psum_scatter(
            acc_qkv[:, width_b : 2 * width_b].astype(jnp.bfloat16),
            "dp",
            scatter_dimension=0,
            tiled=True,
        ).astype(jnp.float32),
        lax.psum_scatter(
            acc_qkv[:, 2 * width_b :].astype(jnp.bfloat16), "dp", scatter_dimension=0, tiled=True
        ).astype(jnp.float32),
        lax.psum_scatter(
            acc_output.astype(jnp.bfloat16), "dp", scatter_dimension=0, tiled=True
        ).astype(jnp.float32),
        lax.psum_scatter(
            acc_inner.astype(jnp.bfloat16), "dp", scatter_dimension=0, tiled=True
        ).astype(jnp.float32),
        lax.psum_scatter(
            acc_outer.astype(jnp.bfloat16), "dp", scatter_dimension=0, tiled=True
        ).astype(jnp.float32),
    )
    norm_parts = lax.psum((acc_gain_one, acc_shift_one, acc_gain_two, acc_shift_two), ("dp", "col"))
    return (
        jnp.stack(outputs),
        jnp.stack(input_grads),
        grad_parts[0],
        grad_parts[1],
        grad_parts[2],
        grad_parts[3],
        grad_parts[4],
        grad_parts[5],
        norm_parts[0],
        norm_parts[1],
        norm_parts[2],
        norm_parts[3],
    )


def solution(mesh):
    placed = (
        P(None, "row", ("dp", "col")),
        P(("row", "dp"), "col"),
        P(("row", "dp"), "col"),
        P(("row", "dp"), "col"),
        P(("col", "dp"), "row"),
        P(("row", "dp"), "col"),
        P(("col", "dp"), "row"),
        P("row"),
        P("row"),
        P("row"),
        P("row"),
        P(),
        P(None, "row", ("dp", "col")),
    )
    return jax.shard_map(
        local,
        mesh=mesh,
        in_specs=placed,
        out_specs=(
            P(None, "row", ("dp", "col")),
            P(None, "row", ("dp", "col")),
            P(("row", "dp"), "col"),
            P(("row", "dp"), "col"),
            P(("row", "dp"), "col"),
            P(("col", "dp"), "row"),
            P(("row", "dp"), "col"),
            P(("col", "dp"), "row"),
            P("row"),
            P("row"),
            P("row"),
            P("row"),
        ),
        check_vma=False,
    )
```

profile of v0, /device:TPU:0, one launch (start us, length us, event | category | flops | bytes accessed | tf_op | source)
XLA Modules:
  0.0 1733.2 jit_solution(12513818273407900545)
XLA Ops:
  56.4 65.9 %reduce-scatter.29.cloned.1.call-done = f32[512,576]{0,1:T(8,128)} async-done(((f32[2048,576]{0,1:T(8,128)}), f32[512,576]{0,1:T(8,128)}) %reduce-scatter.29.cloned.1.call-update) | async-done | bytes 1179664 | tf_op jit(solution)/shard_map/reduce_scatter | solution.py:49
  124.9 28.4 %all_gather.105 = bf16[2048,192]{0,1:T(8,128)(2,1)S(1)} all-gather(bf16[512,192]{0,1:T(8,128)(2,1)S(1)} %slice.241), channel_id=1, replica_groups=mesh['dp'=2,'row'=4,'col'=4] {'row'}, dimensions={0}, use_global_device_ids=true | all-gather | bytes 983040 | tf_op jit(solution)/shard_map/all_gather | solution.py:204
  154.9 64.5 %reduce-scatter.37.cloned.1.call-done = f32[512,576]{0,1:T(8,128)} async-done(((f32[2048,576]{0,1:T(8,128)}), f32[512,576]{0,1:T(8,128)}) %reduce-scatter.37.cloned.1.call-update) | async-done | bytes 1179664 | tf_op jit(solution)/shard_map/reduce_scatter | solution.py:49
  226.7 20.1 %all_gather.104 = bf16[2048,192]{0,1:T(8,128)(2,1)} all-gather(bf16[512,192]{0,1:T(8,128)(2,1)S(1)} %convert_element_type.287), channel_id=1, replica_groups=mesh['dp'=2,'row'=4,'col'=4] {'row'}, dimensions={0}, use_global_device_ids=true | all-gather | bytes 983040 | tf_op jit(solution)/shard_map/all_gather | solution.py:203
  410.6 109.0 %reduce-scatter.33.cloned.1.call-done = f32[512,768]{1,0:T(8,128)} async-done(((f32[2048,768]{1,0:T(8,128)}), f32[512,768]{1,0:T(8,128)}) %reduce-scatter.33.cloned.1.call-update) | async-done | bytes 1572880 | tf_op jit(solution)/shard_map/reduce_scatter | solution.py:49
  533.1 56.2 %all-gather.7.cloned.1.call-done = bf16[2048,768]{1,0:T(8,128)(2,1)} async-done(((bf16[512,768]{1,0:T(8,128)(2,1)}), bf16[2048,768]{1,0:T(8,128)(2,1)}) %all-gather.7.cloned.1.call-update) | async-done | bytes 3145744 | tf_op jit(solution)/shard_map/all_gather | solution.py:45
  594.1 21.3 %reduce-scatter.35.cloned.1.call-done = bf16[512,192]{0,1:T(8,128)(2,1)} async-done(((bf16[2048,192]{0,1:T(8,128)(2,1)}), bf16[512,192]{0,1:T(8,128)(2,1)}) %reduce-scatter.35.cloned.1.call-update) | async-done | bytes 196624 | tf_op jit(solution)/shard_map/reduce_scatter | solution.py:53
  631.0 111.2 %reduce-scatter.41.cloned.1.call-done = f32[512,768]{1,0:T(8,128)} async-done(((f32[2048,768]{1,0:T(8,128)}), f32[512,768]{1,0:T(8,128)}) %reduce-scatter.41.cloned.1.call-update) | async-done | bytes 1572880 | tf_op jit(solution)/shard_map/reduce_scatter | solution.py:49
  748.0 63.9 %all-gather.9.cloned.1.call-done = bf16[2048,768]{1,0:T(8,128)(2,1)} async-done(((bf16[512,768]{1,0:T(8,128)(2,1)}), bf16[2048,768]{1,0:T(8,128)(2,1)}) %all-gather.9.cloned.1.call-update) | async-done | bytes 3145744 | tf_op jit(solution)/shard_map/all_gather | solution.py:45
  817.8 20.1 %reduce-scatter.43.cloned.1.call-done = bf16[512,192]{0,1:T(8,128)(2,1)} async-done(((bf16[2048,192]{0,1:T(8,128)(2,1)}), bf16[512,192]{0,1:T(8,128)(2,1)}) %reduce-scatter.43.cloned.1.call-update) | async-done | bytes 196624 | tf_op jit(solution)/shard_map/reduce_scatter | solution.py:53
  898.0 96.0 %reduce-scatter.57.cloned.1.call-done = f32[512,768]{1,0:T(8,128)} async-done(((f32[2048,768]{1,0:T(8,128)}), f32[512,768]{1,0:T(8,128)}) %reduce-scatter.57.cloned.1.call-update) | async-done | bytes 1572880 | tf_op jit(solution)/shard_map/reduce_scatter | solution.py:49
  997.9 109.5 %reduce-scatter.45.cloned.1.call-done = f32[512,768]{1,0:T(8,128)} async-done(((f32[2048,768]{1,0:T(8,128)}), f32[512,768]{1,0:T(8,128)}) %reduce-scatter.45.cloned.1.call-update) | async-done | bytes 1572880 | tf_op jit(solution)/shard_map/reduce_scatter | solution.py:49
  1111.4 62.2 %all-gather.15.cloned.1.call-done = bf16[2048,768]{1,0:T(8,128)(2,1)} async-done(((bf16[512,768]{1,0:T(8,128)(2,1)}), bf16[2048,768]{1,0:T(8,128)(2,1)}) %all-gather.15.cloned.1.call-update) | async-done | bytes 3145744 | tf_op jit(solution)/shard_map/all_gather | solution.py:45
  1177.6 59.6 %all-gather.11.cloned.1.call-done = bf16[2048,768]{1,0:T(8,128)(2,1)} async-done(((bf16[512,768]{1,0:T(8,128)(2,1)}), bf16[2048,768]{1,0:T(8,128)(2,1)}) %all-gather.11.cloned.1.call-update) | async-done | bytes 3145744 | tf_op jit(solution)/shard_map/all_gather | solution.py:45
  1241.3 20.8 %reduce-scatter.59.cloned.1.call-done = bf16[512,192]{0,1:T(8,128)(2,1)} async-done(((bf16[2048,192]{0,1:T(8,128)(2,1)}), bf16[512,192]{0,1:T(8,128)(2,1)}) %reduce-scatter.59.cloned.1.call-update) | async-done | bytes 196624 | tf_op jit(solution)/shard_map/reduce_scatter | solution.py:53
  1262.1 25.9 %reduce-scatter.47.cloned.1.call-done = bf16[512,192]{0,1:T(8,128)(2,1)} async-done(((bf16[2048,192]{0,1:T(8,128)(2,1)}), bf16[512,192]{0,1:T(8,128)(2,1)}) %reduce-scatter.47.cloned.1.call-update) | async-done | bytes 196624 | tf_op jit(solution)/shard_map/reduce_scatter | solution.py:53
  1331.9 20.8 %reduce-scatter.61.cloned.1.call-done = f32[512,192]{0,1:T(8,128)} async-done(((f32[2048,192]{0,1:T(8,128)}), f32[512,192]{0,1:T(8,128)}) %reduce-scatter.61.cloned.1.call-update) | async-done | bytes 393232 | tf_op jit(solution)/shard_map/reduce_scatter | solution.py:49
  1359.1 30.5 %while.59 = (s32[]{:T(128)}, f32[3,512,64]{1,2,0:T(8,128)}, bf16[3,2048,64]{1,2,0:T(8,128)(2,1)}, bf16[3,2048,64]{1,2,0:T(8,128)(2,1)}, bf16[3,512,64]{2,1,0:T(8...) while((s32[]{:T(128)}, f32[3,512,64]{1,2,0:T(8,128)}, ...), condition=%wide.region_62.63_spmd.clone, body=%wide.region_60.62_spmd.clone.sunk | while | flops 680691200 | bytes 48123144 | solution.py:139
  1392.8 25.2 %while.58 = (s32[]{:T(128)}, f32[3,512,64]{1,2,0:T(8,128)}, bf16[3,2048,64]{1,2,0:T(8,128)(2,1)}, bf16[3,2048,64]{1,2,0:T(8,128)(2,1)S(1)}, bf16[3,512,64]{2,1,0...) while((s32[]{:T(128)}, f32[3,512,64]{1,2,0:T(8,128)}, ...), condition=%wide.region_45.46_spmd.clone, body=%wide.region_43.45_spmd.clone.sunk | while | flops 680691200 | bytes 41045172 | solution.py:139
  1468.7 21.8 %reduce-scatter.65.cloned.1.call-done = bf16[512,192]{0,1:T(8,128)(2,1)} async-done(((bf16[2048,192]{0,1:T(8,128)(2,1)}), bf16[512,192]{0,1:T(8,128)(2,1)}) %reduce-scatter.65.cloned.1.call-update) | async-done | bytes 196624 | tf_op jit(solution)/shard_map/reduce_scatter | solution.py:272
  1504.6 37.7 %all-gather.13.cloned.1.call-done = bf16[2048,576]{0,1:T(8,128)(2,1)} async-done(((bf16[512,576]{0,1:T(8,128)(2,1)}), bf16[2048,576]{0,1:T(8,128)(2,1)}) %all-gather.13.cloned.1.call-update) | async-done | bytes 2359312 | tf_op jit(solution)/shard_map/all_gather | solution.py:45
  1545.0 48.1 %all-gather.17.cloned.1.call-done = bf16[2048,576]{0,1:T(8,128)(2,1)} async-done(((bf16[512,576]{0,1:T(8,128)(2,1)}), bf16[2048,576]{0,1:T(8,128)(2,1)}) %all-gather.17.cloned.1.call-update) | async-done | bytes 2359312 | tf_op jit(solution)/shard_map/all_gather | solution.py:45
  1673.1 25.1 %reduce-scatter.55.cloned.1.call-done = bf16[512,192]{0,1:T(8,128)(2,1)} async-done(((bf16[2048,192]{0,1:T(8,128)(2,1)}), bf16[512,192]{0,1:T(8,128)(2,1)}) %reduce-scatter.55.cloned.1.call-update) | async-done | bytes 196624 | tf_op jit(solution)/shard_map/reduce_scatter | solution.py:53
  1698.2 25.9 %reduce-scatter.67.cloned.1.call-done = bf16[512,192]{0,1:T(8,128)(2,1)} async-done(((bf16[2048,192]{0,1:T(8,128)(2,1)}), bf16[512,192]{0,1:T(8,128)(2,1)}) %reduce-scatter.67.cloned.1.call-update) | async-done | bytes 196624 | tf_op jit(solution)/shard_map/reduce_scatter | solution.py:53
  (511 shorter events, 634.2 us)
Async XLA Ops:
  7.2 115.1 %reduce-scatter.29.cloned.1.call-start = ((), (), s32[]{:S(2)}) async-start(), calls=%async_computation.26 | async-start | bytes 5898240 | tf_op jit(solution)/shard_map/reduce_scatter | solution.py:49
  36.5 182.9 %reduce-scatter.37.cloned.1.call-start = ((), (), s32[]{:S(2)}) async-start(), calls=%async_computation.31 | async-start | bytes 5898240 | tf_op jit(solution)/shard_map/reduce_scatter | solution.py:49
  48.4 316.8 %reduce-scatter.31.cloned.1.call-start = ((), (), s32[]{:S(2)}) async-start(), calls=%async_computation.27 | async-start | bytes 983040 | tf_op jit(solution)/shard_map/reduce_scatter | solution.py:53
  358.0 161.6 %reduce-scatter.33.cloned.1.call-start = ((), (), s32[]{:S(2)}) async-start(), calls=%async_computation.28 | async-start | bytes 7864320 | tf_op jit(solution)/shard_map/reduce_scatter | solution.py:49
  410.6 178.7 %all-gather.7.cloned.1.call-start = ((), (), s32[]{:S(2)}) async-start(), calls=%async_computation.29 | async-start | bytes 3932160 | tf_op jit(solution)/shard_map/all_gather | solution.py:45
  525.1 90.2 %reduce-scatter.35.cloned.1.call-start = ((), (), s32[]{:S(2)}) async-start(), calls=%async_computation.30 | async-start | bytes 983040 | tf_op jit(solution)/shard_map/reduce_scatter | solution.py:53
  593.3 148.9 %reduce-scatter.41.cloned.1.call-start = ((), (), s32[]{:S(2)}) async-start(), calls=%async_computation.33 | async-start | bytes 7864320 | tf_op jit(solution)/shard_map/reduce_scatter | solution.py:49
  630.9 181.0 %all-gather.9.cloned.1.call-start = ((), (), s32[]{:S(2)}) async-start(), calls=%async_computation.34 | async-start | bytes 3932160 | tf_op jit(solution)/shard_map/all_gather | solution.py:45
  747.7 90.2 %reduce-scatter.43.cloned.1.call-start = ((), (), s32[]{:S(2)}) async-start(), calls=%async_computation.35 | async-start | bytes 983040 | tf_op jit(solution)/shard_map/reduce_scatter | solution.py:53
  815.8 178.1 %reduce-scatter.57.cloned.1.call-start = ((), (), s32[]{:S(2)}) async-start(), calls=%async_computation.44 | async-start | bytes 7864320 | tf_op jit(solution)/shard_map/reduce_scatter | solution.py:49
  883.4 224.0 %reduce-scatter.45.cloned.1.call-start = ((), (), s32[]{:S(2)}) async-start(), calls=%async_computation.36 | async-start | bytes 7864320 | tf_op jit(solution)/shard_map/reduce_scatter | solution.py:49
  897.9 275.7 %all-gather.15.cloned.1.call-start = ((), (), s32[]{:S(2)}) async-start(), calls=%async_computation.45 | async-start | bytes 3932160 | tf_op jit(solution)/shard_map/all_gather | solution.py:45
  997.8 239.4 %all-gather.11.cloned.1.call-start = ((), (), s32[]{:S(2)}) async-start(), calls=%async_computation.37 | async-start | bytes 3932160 | tf_op jit(solution)/shard_map/all_gather | solution.py:45
  1111.3 150.8 %reduce-scatter.59.cloned.1.call-start = ((), (), s32[]{:S(2)}) async-start(), calls=%async_computation.46 | async-start | bytes 983040 | tf_op jit(solution)/shard_map/reduce_scatter | solution.py:53
  1177.6 110.3 %reduce-scatter.47.cloned.1.call-start = ((), (), s32[]{:S(2)}) async-start(), calls=%async_computation.38 | async-start | bytes 983040 | tf_op jit(solution)/shard_map/reduce_scatter | solution.py:53
  1241.2 111.6 %reduce-scatter.61.cloned.1.call-start = ((), (), s32[]{:S(2)}) async-start(), calls=%async_computation.47 | async-start | bytes 1966080 | tf_op jit(solution)/shard_map/reduce_scatter | solution.py:49
  1419.7 122.6 %all-gather.13.cloned.1.call-start = ((), (), s32[]{:S(2)}) async-start(), calls=%async_computation.42 | async-start | bytes 2949120 | tf_op jit(solution)/shard_map/all_gather | solution.py:45
  1467.3 125.8 %all-gather.17.cloned.1.call-start = ((), (), s32[]{:S(2)}) async-start(), calls=%async_computation.50 | async-start | bytes 2949120 | tf_op jit(solution)/shard_map/all_gather | solution.py:45
  1492.3 115.1 %reduce-scatter.79.cloned.1.call-start = ((), (), s32[]{:S(2)}) async-start(), calls=%async_computation.57 | async-start | bytes 589824
  1497.1 125.0 %reduce-scatter.77.cloned.1.call-start = ((), (), s32[]{:S(2)}) async-start(), calls=%async_computation.56 | async-start | bytes 442368 | tf_op jit(solution)/shard_map/reduce_scatter | solution.py:303
  1502.2 134.9 %reduce-scatter.75.cloned.1.call-start = ((), (), s32[]{:S(2)}) async-start(), calls=%async_computation.55 | async-start | bytes 147456 | tf_op jit(solution)/shard_map/reduce_scatter | solution.py:300
  1504.6 142.6 %reduce-scatter.69.cloned.1.call-start = ((), (), s32[]{:S(2)}) async-start(), calls=%async_computation.52 | async-start | bytes 147456 | tf_op jit(solution)/shard_map/reduce_scatter | solution.py:288
  1598.0 100.3 %reduce-scatter.55.cloned.1.call-start = ((), (), s32[]{:S(2)}) async-start(), calls=%async_computation.43 | async-start | bytes 983040 | tf_op jit(solution)/shard_map/reduce_scatter | solution.py:53
  1601.6 122.5 %reduce-scatter.67.cloned.1.call-start = ((), (), s32[]{:S(2)}) async-start(), calls=%async_computation.51 | async-start | bytes 983040 | tf_op jit(solution)/shard_map/reduce_scatter | solution.py:53
  (109 other events, 2679.2 us)
Sparse Core Ops, SparseCore 0:
  36.6 85.5 reduce-scatter.28
  124.5 94.8 reduce-scatter.36
  320.4 24.0 reduce-scatter.30
  358.1 24.0 reduce-scatter.38
  410.7 108.8 reduce-scatter.32
  525.3 63.9 all-gather.6
  631.0 111.1 reduce-scatter.40
  747.8 63.9 all-gather.8
  816.0 21.9 reduce-scatter.42
  883.5 110.3 reduce-scatter.56
  996.1 111.2 reduce-scatter.44
  1109.5 64.0 all-gather.14
  1175.0 62.1 all-gather.10
  1264.6 23.2 reduce-scatter.46
  1319.3 33.4 reduce-scatter.60
  1354.9 34.2 reduce-scatter.48
  1391.5 22.2 reduce-scatter.62
  1418.2 22.4 reduce-scatter.50
  1442.9 22.5 reduce-scatter.52
  1467.8 22.5 reduce-scatter.64
  1492.6 49.6 all-gather.12
  1543.7 49.3 all-gather.16
  1674.9 23.2 reduce-scatter.54
  1700.8 23.2 reduce-scatter.66
  (8 shorter events, 107.2 us)
where the time goes:
time: 1740 us; the launch traced here: 1730 us
  waiting for transfers between devices  1170 us (67%)
  blocking collectives  278 us (16%)
  matrix products  123 us (7%)
  other arithmetic  93 us (5%)
  local copies, waits for them, and re-layouts  54.1 us (3%)
    reduce_scatter x8, waiting for transfers between devices, reduce_rows(): return lax.psum_scatter(values, 'row', scatter_dimension=0, tiled=True)  577 us
    all_gather x6, waiting for transfers between devices, along_row(): return lax.all_gather(values, 'row', axis=0, tiled=True)  328 us
    reduce_scatter x8, waiting for transfers between devices, reduce_cols(): lax.psum_scatter(values.astype(jnp.bfloat16), 'col', scatter_dimension=0,...  156 us
    all_gather x8, blocking collectives, along_col(): return lax.all_gather(values, 'col', axis=0, tiled=True)  66.9 us
    dot_general x26, matrix products, times_transpose(): lax.dot_general(left, right, (((1,), (1,)), ((), ())), preferred_element_...  52.3 us
    psum x4, blocking collectives, feature_totals(): return lax.psum((first_sum, second_sum), 'row')  46.8 us
    all_gather x2, blocking collectives, local(): lax.all_gather(value_low, 'row', axis=0, tiled=True)  45.8 us
    reduce_scatter x2, waiting for transfers between devices, local(): lax.psum_scatter(merge_heads(grad_v_heads).astype(jnp.bfloat16), 'row', s...  41.3 us
  transfers between devices with their start and end apart: 32, of which 28 were waited for; matrix products, arithmetic and copies ran while one was open for 9% of the time, Pallas kernels for 0%

commit v1 on v0

--- a/solution.py
+++ b/solution.py
@@ -6,6 +6,27 @@
 HD = 64
 norm_eps = 1e-05
 masked_score = -1e30
+
+
+def in_order(blocks, dim):
+    blocks = jnp.moveaxis(blocks, 0, dim)
+    shape = blocks.shape
+    return blocks.reshape(*shape[:dim], shape[dim] * shape[dim + 1], *shape[dim + 2 :])
+
+
+def collected_by_bits(array, axis):
+    count, index = (lax.axis_size(axis), lax.axis_index(axis))
+    parts, bit = (array[None], 1)
+    while bit < count:
+        other = lax.ppermute(parts, axis, [(i, i ^ bit) for i in range(count)])
+        low = index & bit == 0
+        parts = jnp.concatenate([jnp.where(low, parts, other), jnp.where(low, other, parts)])
+        bit *= 2
+    return parts
+
+
+def doubled_up(x, axis, dim):
+    return in_order(collected_by_bits(x, axis), dim)
 
 
 def rotate_pairs(values, positions, head_size, direction):
@@ -201,7 +222,7 @@
         value_low = projected[:, 2 * width_b :].astype(jnp.bfloat16)
         key_all, value_all = (
             lax.all_gather(key_rot, "row", axis=0, tiled=True),
-            lax.all_gather(value_low, "row", axis=0, tiled=True),
+            doubled_up(value_low, "row", 0),
         )
         query_heads = split_heads(query_rot, head_size)
         head_outs, log_totals = attend_forward(

time: 1740 us -> 1800 us (1.034)
  blocking collectives: 278 us -> 310 us
    all_gather x2, blocking collectives: 37.5 us -> 58.8 us  [local(): lax.all_gather(key_rot, 'row', axis=0, tiled=True)]
  transfers between devices with their start and end apart: 32 -> 36, of which waited for: 28 -> 27; matrix products, arithmetic and copies ran while one was open for 9% -> 10% of each run, Pallas kernels for 0% -> 0%
where the time goes in v1:
time: 1800 us; the launch traced here: 1790 us
  waiting for transfers between devices  1160 us (64%)
  blocking collectives  310 us (17%)
  matrix products  122 us (7%)
  other arithmetic  99 us (6%)
  local copies, waits for them, and re-layouts  70.3 us (4%)
    reduce_scatter x8, waiting for transfers between devices, reduce_rows(): return lax.psum_scatter(values, 'row', scatter_dimension=0, tiled=True)  574 us
    all_gather x6, waiting for transfers between devices, along_row(): return lax.all_gather(values, 'row', axis=0, tiled=True)  328 us
    reduce_scatter x8, waiting for transfers between devices, reduce_cols(): lax.psum_scatter(values.astype(jnp.bfloat16), 'col', scatter_dimension=0,...  154 us
    all_gather x8, blocking collectives, along_col(): return lax.all_gather(values, 'col', axis=0, tiled=True)  66.7 us
    all_gather x2, blocking collectives, local(): lax.all_gather(key_rot, 'row', axis=0, tiled=True)  58.8 us
    dot_general x26, matrix products, times_transpose(): lax.dot_general(left, right, (((1,), (1,)), ((), ())), preferred_element_...  52.5 us
    all_gather x2, blocking collectives, local(): lax.all_gather(value_low, 'row', axis=0, tiled=True)  52.4 us
    psum x4, blocking collectives, feature_totals(): return lax.psum((first_sum, second_sum), 'row')  46.8 us
  transfers between devices with their start and end apart: 36, of which 27 were waited for; matrix products, arithmetic and copies ran while one was open for 10% of the time, Pallas kernels for 0%

profile of v1, /device:TPU:0, one launch (start us, length us, event | category | flops | bytes accessed | tf_op | source)
XLA Modules:
  0.0 1788.6 jit_solution(719556727810100772)
XLA Ops:
  56.2 66.0 %reduce-scatter.29.cloned.1.call-done = f32[512,576]{0,1:T(8,128)} async-done(((f32[2048,576]{0,1:T(8,128)}), f32[512,576]{0,1:T(8,128)}) %reduce-scatter.29.cloned.1.call-update) | async-done | bytes 1179664 | tf_op jit(solution)/shard_map/reduce_scatter | solution.py:70
  127.0 83.3 %reduce-scatter.37.cloned.1.call-done = f32[512,576]{0,1:T(8,128)} async-done(((f32[2048,576]{0,1:T(8,128)}), f32[512,576]{0,1:T(8,128)}) %reduce-scatter.37.cloned.1.call-update) | async-done | bytes 1179664 | tf_op jit(solution)/shard_map/reduce_scatter | solution.py:70
  248.5 39.7 %all_gather.102 = bf16[2048,192]{0,1:T(8,128)(2,1)} all-gather(bf16[512,192]{0,1:T(8,128)(2,1)S(1)} %copy-done.60), channel_id=1, replica_groups=mesh['dp'=2,'row'=4,'col'=4] {'row'}, dimensions={0}, use_global_device_ids=true | all-gather | bytes 983040 | tf_op jit(solution)/shard_map/all_gather | solution.py:224
  428.1 108.8 %reduce-scatter.33.cloned.1.call-done = f32[512,768]{1,0:T(8,128)} async-done(((f32[2048,768]{1,0:T(8,128)}), f32[512,768]{1,0:T(8,128)}) %reduce-scatter.33.cloned.1.call-update) | async-done | bytes 1572880 | tf_op jit(solution)/shard_map/reduce_scatter | solution.py:70
  550.4 56.2 %all-gather.7.cloned.1.call-done = bf16[2048,768]{1,0:T(8,128)(2,1)} async-done(((bf16[512,768]{1,0:T(8,128)(2,1)}), bf16[2048,768]{1,0:T(8,128)(2,1)}) %all-gather.7.cloned.1.call-update) | async-done | bytes 3145744 | tf_op jit(solution)/shard_map/all_gather | solution.py:66
  611.3 21.3 %reduce-scatter.35.cloned.1.call-done = bf16[512,192]{0,1:T(8,128)(2,1)} async-done(((bf16[2048,192]{0,1:T(8,128)(2,1)}), bf16[512,192]{0,1:T(8,128)(2,1)}) %reduce-scatter.35.cloned.1.call-update) | async-done | bytes 196624 | tf_op jit(solution)/shard_map/reduce_scatter | solution.py:74
  648.3 111.2 %reduce-scatter.41.cloned.1.call-done = f32[512,768]{1,0:T(8,128)} async-done(((f32[2048,768]{1,0:T(8,128)}), f32[512,768]{1,0:T(8,128)}) %reduce-scatter.41.cloned.1.call-update) | async-done | bytes 1572880 | tf_op jit(solution)/shard_map/reduce_scatter | solution.py:70
  765.1 64.1 %all-gather.9.cloned.1.call-done = bf16[2048,768]{1,0:T(8,128)(2,1)} async-done(((bf16[512,768]{1,0:T(8,128)(2,1)}), bf16[2048,768]{1,0:T(8,128)(2,1)}) %all-gather.9.cloned.1.call-update) | async-done | bytes 3145744 | tf_op jit(solution)/shard_map/all_gather | solution.py:66
  834.9 20.3 %reduce-scatter.43.cloned.1.call-done = bf16[512,192]{0,1:T(8,128)(2,1)} async-done(((bf16[2048,192]{0,1:T(8,128)(2,1)}), bf16[512,192]{0,1:T(8,128)(2,1)}) %reduce-scatter.43.cloned.1.call-update) | async-done | bytes 196624 | tf_op jit(solution)/shard_map/reduce_scatter | solution.py:74
  915.4 95.9 %reduce-scatter.57.cloned.1.call-done = f32[512,768]{1,0:T(8,128)} async-done(((f32[2048,768]{1,0:T(8,128)}), f32[512,768]{1,0:T(8,128)}) %reduce-scatter.57.cloned.1.call-update) | async-done | bytes 1572880 | tf_op jit(solution)/shard_map/reduce_scatter | solution.py:70
  1015.6 109.1 %reduce-scatter.45.cloned.1.call-done = f32[512,768]{1,0:T(8,128)} async-done(((f32[2048,768]{1,0:T(8,128)}), f32[512,768]{1,0:T(8,128)}) %reduce-scatter.45.cloned.1.call-update) | async-done | bytes 1572880 | tf_op jit(solution)/shard_map/reduce_scatter | solution.py:70
  1128.7 62.2 %all-gather.15.cloned.1.call-done = bf16[2048,768]{1,0:T(8,128)(2,1)} async-done(((bf16[512,768]{1,0:T(8,128)(2,1)}), bf16[2048,768]{1,0:T(8,128)(2,1)}) %all-gather.15.cloned.1.call-update) | async-done | bytes 3145744 | tf_op jit(solution)/shard_map/all_gather | solution.py:66
  1195.0 59.6 %all-gather.11.cloned.1.call-done = bf16[2048,768]{1,0:T(8,128)(2,1)} async-done(((bf16[512,768]{1,0:T(8,128)(2,1)}), bf16[2048,768]{1,0:T(8,128)(2,1)}) %all-gather.11.cloned.1.call-update) | async-done | bytes 3145744 | tf_op jit(solution)/shard_map/all_gather | solution.py:66
  1258.6 20.8 %reduce-scatter.59.cloned.1.call-done = bf16[512,192]{0,1:T(8,128)(2,1)} async-done(((bf16[2048,192]{0,1:T(8,128)(2,1)}), bf16[512,192]{0,1:T(8,128)(2,1)}) %reduce-scatter.59.cloned.1.call-update) | async-done | bytes 196624 | tf_op jit(solution)/shard_map/reduce_scatter | solution.py:74
  1279.4 25.9 %reduce-scatter.47.cloned.1.call-done = bf16[512,192]{0,1:T(8,128)(2,1)} async-done(((bf16[2048,192]{0,1:T(8,128)(2,1)}), bf16[512,192]{0,1:T(8,128)(2,1)}) %reduce-scatter.47.cloned.1.call-update) | async-done | bytes 196624 | tf_op jit(solution)/shard_map/reduce_scatter | solution.py:74
  1337.6 29.0 %all_gather.117 = bf16[2048,192]{0,1:T(8,128)(2,1)} all-gather(bf16[512,192]{0,1:T(8,128)(2,1)S(1)} %slice.241), channel_id=1, replica_groups=mesh['dp'=2,'row'=4,'col'=4] {'row'}, dimensions={0}, use_global_device_ids=true | all-gather | bytes 983040 | tf_op jit(solution)/shard_map/all_gather | solution.py:275
  1370.1 23.5 %all_gather.122 = bf16[2048,192]{0,1:T(8,128)(2,1)} all-gather(bf16[512,192]{0,1:T(8,128)(2,1)S(1)} %slice.240), channel_id=1, replica_groups=mesh['dp'=2,'row'=4,'col'=4] {'row'}, dimensions={0}, use_global_device_ids=true | all-gather | bytes 983040 | tf_op jit(solution)/shard_map/all_gather | solution.py:275
  1414.5 30.3 %while.59 = (s32[]{:T(128)}, f32[3,512,64]{1,2,0:T(8,128)}, bf16[3,2048,64]{1,2,0:T(8,128)(2,1)}, bf16[3,2048,64]{1,2,0:T(8,128)(2,1)}, bf16[3,512,64]{2,1,0:T(8...) while((s32[]{:T(128)}, f32[3,512,64]{1,2,0:T(8,128)}, ...), condition=%wide.region_62.63_spmd.clone, body=%wide.region_60.62_spmd.clone.sunk | while | flops 680691200 | bytes 48123144 | solution.py:160
  1448.2 24.9 %while.58 = (s32[]{:T(128)}, f32[3,512,64]{1,2,0:T(8,128)}, bf16[3,2048,64]{1,2,0:T(8,128)(2,1)}, bf16[3,2048,64]{1,2,0:T(8,128)(2,1)S(1)}, bf16[3,512,64]{2,1,0...) while((s32[]{:T(128)}, f32[3,512,64]{1,2,0:T(8,128)}, ...), condition=%wide.region_45.46_spmd.clone, body=%wide.region_43.45_spmd.clone.sunk | while | flops 680691200 | bytes 41045172 | solution.py:160
  1523.8 21.9 %reduce-scatter.65.cloned.1.call-done = bf16[512,192]{0,1:T(8,128)(2,1)} async-done(((bf16[2048,192]{0,1:T(8,128)(2,1)}), bf16[512,192]{0,1:T(8,128)(2,1)}) %reduce-scatter.65.cloned.1.call-update) | async-done | bytes 196624 | tf_op jit(solution)/shard_map/reduce_scatter | solution.py:293
  1560.2 37.4 %all-gather.13.cloned.1.call-done = bf16[2048,576]{0,1:T(8,128)(2,1)} async-done(((bf16[512,576]{0,1:T(8,128)(2,1)}), bf16[2048,576]{0,1:T(8,128)(2,1)}) %all-gather.13.cloned.1.call-update) | async-done | bytes 2359312 | tf_op jit(solution)/shard_map/all_gather | solution.py:66
  1600.4 48.1 %all-gather.17.cloned.1.call-done = bf16[2048,576]{0,1:T(8,128)(2,1)} async-done(((bf16[512,576]{0,1:T(8,128)(2,1)}), bf16[2048,576]{0,1:T(8,128)(2,1)}) %all-gather.17.cloned.1.call-update) | async-done | bytes 2359312 | tf_op jit(solution)/shard_map/all_gather | solution.py:66
  1728.5 25.1 %reduce-scatter.55.cloned.1.call-done = bf16[512,192]{0,1:T(8,128)(2,1)} async-done(((bf16[2048,192]{0,1:T(8,128)(2,1)}), bf16[512,192]{0,1:T(8,128)(2,1)}) %reduce-scatter.55.cloned.1.call-update) | async-done | bytes 196624 | tf_op jit(solution)/shard_map/reduce_scatter | solution.py:74
  1753.6 25.9 %reduce-scatter.67.cloned.1.call-done = bf16[512,192]{0,1:T(8,128)(2,1)} async-done(((bf16[2048,192]{0,1:T(8,128)(2,1)}), bf16[512,192]{0,1:T(8,128)(2,1)}) %reduce-scatter.67.cloned.1.call-update) | async-done | bytes 196624 | tf_op jit(solution)/shard_map/reduce_scatter | solution.py:74
  (550 shorter events, 649.2 us)
Async XLA Ops:
  7.2 115.0 %reduce-scatter.29.cloned.1.call-start = ((), (), s32[]{:S(2)}) async-start(), calls=%async_computation.26 | async-start | bytes 5898240 | tf_op jit(solution)/shard_map/reduce_scatter | solution.py:70
  36.4 173.9 %reduce-scatter.37.cloned.1.call-start = ((), (), s32[]{:S(2)}) async-start(), calls=%async_computation.31 | async-start | bytes 5898240 | tf_op jit(solution)/shard_map/reduce_scatter | solution.py:70
  48.4 336.0 %reduce-scatter.39.cloned.1.call-start = ((), (), s32[]{:S(2)}) async-start(), calls=%async_computation.32 | async-start | bytes 983040 | tf_op jit(solution)/shard_map/reduce_scatter | solution.py:74
  123.9 114.5 %collective-permute-start = (bf16[1,512,192]{1,2,0:T(8,128)(2,1)}, bf16[1,512,192]{1,2,0:T(8,128)(2,1)}, u32[]{:S(2)}, u32[]{:S(2)}) collective-permute-start(bf16[1,512,192]{1,2,0:T(8,128)(2,1)} %slice_bitcast_fusion.2), channel_id=1, source_target_pairs={{0,4},{4,0},{8,12},{12,8},{1,5},{5,1},{9,13},{13,9},{2,6},{6,2},{1... | collective-permute-start | bytes 589832 | tf_op jit(solution)/shard_map/ppermute | solution.py:21
  377.2 159.6 %reduce-scatter.33.cloned.1.call-start = ((), (), s32[]{:S(2)}) async-start(), calls=%async_computation.28 | async-start | bytes 7864320 | tf_op jit(solution)/shard_map/reduce_scatter | solution.py:70
  427.8 178.8 %all-gather.7.cloned.1.call-start = ((), (), s32[]{:S(2)}) async-start(), calls=%async_computation.29 | async-start | bytes 3932160 | tf_op jit(solution)/shard_map/all_gather | solution.py:66
  610.5 149.0 %reduce-scatter.41.cloned.1.call-start = ((), (), s32[]{:S(2)}) async-start(), calls=%async_computation.33 | async-start | bytes 7864320 | tf_op jit(solution)/shard_map/reduce_scatter | solution.py:70
  648.2 181.0 %all-gather.9.cloned.1.call-start = ((), (), s32[]{:S(2)}) async-start(), calls=%async_computation.34 | async-start | bytes 3932160 | tf_op jit(solution)/shard_map/all_gather | solution.py:66
  833.2 178.1 %reduce-scatter.57.cloned.1.call-start = ((), (), s32[]{:S(2)}) async-start(), calls=%async_computation.44 | async-start | bytes 7864320 | tf_op jit(solution)/shard_map/reduce_scatter | solution.py:70
  900.8 224.0 %reduce-scatter.45.cloned.1.call-start = ((), (), s32[]{:S(2)}) async-start(), calls=%async_computation.36 | async-start | bytes 7864320 | tf_op jit(solution)/shard_map/reduce_scatter | solution.py:70
  915.4 275.6 %all-gather.15.cloned.1.call-start = ((), (), s32[]{:S(2)}) async-start(), calls=%async_computation.45 | async-start | bytes 3932160 | tf_op jit(solution)/shard_map/all_gather | solution.py:66
  1015.2 239.4 %all-gather.11.cloned.1.call-start = ((), (), s32[]{:S(2)}) async-start(), calls=%async_computation.37 | async-start | bytes 3932160 | tf_op jit(solution)/shard_map/all_gather | solution.py:66
  1128.6 150.8 %reduce-scatter.59.cloned.1.call-start = ((), (), s32[]{:S(2)}) async-start(), calls=%async_computation.46 | async-start | bytes 983040 | tf_op jit(solution)/shard_map/reduce_scatter | solution.py:74
  1194.9 110.3 %reduce-scatter.47.cloned.1.call-start = ((), (), s32[]{:S(2)}) async-start(), calls=%async_computation.38 | async-start | bytes 983040 | tf_op jit(solution)/shard_map/reduce_scatter | solution.py:74
  1258.5 149.7 %reduce-scatter.61.cloned.1.call-start = ((), (), s32[]{:S(2)}) async-start(), calls=%async_computation.47 | async-start | bytes 1966080 | tf_op jit(solution)/shard_map/reduce_scatter | solution.py:70
  1336.5 108.5 %reduce-scatter.49.cloned.1.call-start = ((), (), s32[]{:S(2)}) async-start(), calls=%async_computation.39 | async-start | bytes 1966080 | tf_op jit(solution)/shard_map/reduce_scatter | solution.py:70
  1474.8 122.9 %all-gather.13.cloned.1.call-start = ((), (), s32[]{:S(2)}) async-start(), calls=%async_computation.42 | async-start | bytes 2949120 | tf_op jit(solution)/shard_map/all_gather | solution.py:66
  1522.7 125.8 %all-gather.17.cloned.1.call-start = ((), (), s32[]{:S(2)}) async-start(), calls=%async_computation.50 | async-start | bytes 2949120 | tf_op jit(solution)/shard_map/all_gather | solution.py:66
  1547.6 115.1 %reduce-scatter.79.cloned.1.call-start = ((), (), s32[]{:S(2)}) async-start(), calls=%async_computation.57 | async-start | bytes 589824
  1552.5 125.1 %reduce-scatter.77.cloned.1.call-start = ((), (), s32[]{:S(2)}) async-start(), calls=%async_computation.56 | async-start | bytes 442368 | tf_op jit(solution)/shard_map/reduce_scatter | solution.py:324
  1557.6 135.0 %reduce-scatter.75.cloned.1.call-start = ((), (), s32[]{:S(2)}) async-start(), calls=%async_computation.55 | async-start | bytes 147456 | tf_op jit(solution)/shard_map/reduce_scatter | solution.py:321
  1560.0 142.6 %reduce-scatter.69.cloned.1.call-start = ((), (), s32[]{:S(2)}) async-start(), calls=%async_computation.52 | async-start | bytes 147456 | tf_op jit(solution)/shard_map/reduce_scatter | solution.py:309
  1653.4 100.3 %reduce-scatter.55.cloned.1.call-start = ((), (), s32[]{:S(2)}) async-start(), calls=%async_computation.43 | async-start | bytes 983040 | tf_op jit(solution)/shard_map/reduce_scatter | solution.py:74
  1657.0 122.5 %reduce-scatter.67.cloned.1.call-start = ((), (), s32[]{:S(2)}) async-start(), calls=%async_computation.51 | async-start | bytes 983040 | tf_op jit(solution)/shard_map/reduce_scatter | solution.py:74
  (122 other events, 2968.0 us)
Sparse Core Ops, SparseCore 0:
  36.6 85.5 reduce-scatter.28
  124.5 85.7 reduce-scatter.36
  335.6 22.5 reduce-scatter.38
  377.3 21.9 reduce-scatter.30
  427.9 108.9 reduce-scatter.32
  542.5 63.9 all-gather.6
  648.3 111.1 reduce-scatter.40
  765.1 64.0 all-gather.8
  833.3 21.9 reduce-scatter.42
  900.9 110.3 reduce-scatter.56
  1013.4 111.2 reduce-scatter.44
  1126.9 64.0 all-gather.14
  1192.4 62.1 all-gather.10
  1282.0 23.2 reduce-scatter.46
  1336.7 50.1 reduce-scatter.60
  1408.2 34.7 reduce-scatter.48
  1445.3 22.3 reduce-scatter.62
  1473.3 22.6 reduce-scatter.50
  1498.3 22.5 reduce-scatter.52
  1523.2 22.5 reduce-scatter.64
  1547.9 49.6 all-gather.12
  1599.1 49.3 all-gather.16
  1730.3 23.2 reduce-scatter.54
  1756.2 23.2 reduce-scatter.66
  (8 shorter events, 107.2 us)
